TPU v7x, 256 devices: a whole 4x4x8 slice. The times are simulated.
256 devices in a mesh: dp: 8 (over x, core), code: 32 (over z, y).
Axes of the slice: x: 4, y: 4, z: 8, core: 2. Of those that a mesh axis runs over, the one named last changes fastest.
Arguments:
- latents: bfloat16 [4096, 256], P(('dp', 'code')), may hold values from -1000 to 1000
- out_grad: bfloat16 [4096, 256], P(('dp', 'code')), may hold values from -6 to 6
- targets: int32 [4096], P('dp'), may hold values from 0 to 262143
- codebook: bfloat16 [262144, 256], P('code'), may hold values from -2 to 2
Outputs:
- latent_grad: bfloat16 [4096, 256], P(('dp', 'code'))
- codebook_grad: float32 [262144, 256], P(('code', 'dp'))
- token_loss: float32 [4096], P(('dp', 'code'))
All inputs are finite; a program needn't handle non-finite values.
Results may differ from a plain program's by a relative error of at most 0.0042.
Values may be sent and summed in bfloat16 or wider, within the bound.
No kernel may reach another device: no remote copies, remote signals or barrier semaphores. Data moves between devices by JAX's collectives and lax.ppermute only.
A program may use at most 128 MiB of HBM per device.

v0:
```python
import functools

import jax
import jax.numpy as jnp
from jax import lax
from jax.experimental import pallas as pl
from jax.experimental.pallas import tpu as pltpu
from jax.sharding import Mesh
from jax.sharding import PartitionSpec as P

ce_weight = 1.0
F32 = jnp.float32
BF16 = jnp.bfloat16
NT = (((1,), (1,)), ((), ()))
NN = (((1,), (0,)), ((), ()))
ZY = ("z", "y")
XC = ("x", "core")
VMEM_LIMIT = 32 << 20


def dot(a, b, dims, precision=None):
    return lax.dot_general(a, b, dims, preferred_element_type=F32, precision=precision)


def params(**kw):
    return pltpu.CompilerParams(vmem_limit_bytes=VMEM_LIMIT, **kw)


def cost(flops, bytes_accessed, trans=0):
    return pl.CostEstimate(flops=flops, bytes_accessed=bytes_accessed, transcendentals=trans)


def pick_kernel(cb, tgt_ref, book_ref, out_ref):
    i = pl.program_id(0)

    @pl.when(i == 0)
    def _():
        out_ref[...] = jnp.zeros_like(out_ref)

    tokens = tgt_ref.shape[0]
    ids = lax.broadcasted_iota(jnp.int32, (tokens, cb), 1) + i * cb
    hit = jnp.where(ids == tgt_ref[:, :1], 1.0, 0.0).astype(BF16)
    out_ref[...] += dot(hit, book_ref[...], NN)


def pick_rows(tgt_cols, book):
    tokens, codes, d = tgt_cols.shape[0], *book.shape
    cb = 2048
    return pl.pallas_call(
        functools.partial(pick_kernel, cb),
        grid=(codes // cb,),
        in_specs=[
            pl.BlockSpec((tokens, 128), lambda i: (0, 0)),
            pl.BlockSpec((cb, d), lambda i: (i, 0)),
        ],
        out_specs=pl.BlockSpec((tokens, d), lambda i: (0, 0)),
        out_shape=pltpu.HBM((tokens, d), F32),
        compiler_params=params(),
        cost_estimate=cost(2 * tokens * codes * d, codes * d * 2),
        name="pick",
    )(tgt_cols, book)


def fold(x):
    return sum(x[:, i : i + 128] for i in range(0, x.shape[1], 128))


def as_row(x):
    return jnp.sum(x.T, axis=0, keepdims=True)


def as_cols(row):
    return jnp.broadcast_to(row, (128, row.shape[1])).T


def stats_kernel(
    steps, sub, lat_ref, grad_ref, book_ref, rows_hbm, out_ref, m_s, l_s, w_s, rows_ref, sem
):
    i = pl.program_id(0)
    load = pltpu.make_async_copy(rows_hbm, rows_ref, sem)

    @pl.when(i == 0)
    def _():
        load.start()
        m_s[...] = jnp.full_like(m_s, -jnp.inf)
        l_s[...] = jnp.zeros_like(l_s)
        w_s[...] = jnp.zeros_like(w_s)

    cb, tokens = book_ref.shape[0], lat_ref.shape[0]
    count = cb // sub

    def scores(ref, j):
        return dot(book_ref[j * sub : (j + 1) * sub, :], ref[...], NT).reshape(sub // 8, 8, tokens)

    m, l, w = m_s[...], l_s[...], w_s[...]
    ahead = scores(lat_ref, 0)
    for j in range(count):
        logit = ahead
        if j + 1 < count:
            ahead = scores(lat_ref, j + 1)
        back = scores(grad_ref, j)
        new = jnp.maximum(m, jnp.max(logit, axis=0))
        factor = jnp.exp(m - new)
        expo = jnp.exp(logit - new[None])
        l = l * factor + jnp.sum(expo, axis=0)
        w = w * factor + jnp.sum(expo * back, axis=0)
        m = new
    m_s[...], l_s[...], w_s[...] = m, l, w

    @pl.when(i == steps - 1)
    def _():
        m = m_s[...]
        top = jnp.max(m, axis=0, keepdims=True)
        scale = jnp.exp(m - top)
        total = jnp.sum(l_s[...] * scale, axis=0, keepdims=True)
        weighted = jnp.sum(w_s[...] * scale, axis=0, keepdims=True)
        load.wait()
        picked = as_row(fold(lat_ref[...].astype(F32) * rows_ref[...]))
        pack = jnp.concatenate([top, total, weighted, picked], axis=0)
        out_ref[...] = jnp.broadcast_to(pack[None], out_ref.shape)


def local_stats(toks, rows, book, peers, cb=4096, sub=512):
    tokens, (codes, d) = toks.shape[0], book.shape
    steps = codes // cb
    return pl.pallas_call(
        functools.partial(stats_kernel, steps, sub),
        grid=(steps,),
        in_specs=[
            pl.BlockSpec((tokens, d), lambda i: (0, 0)),
            pl.BlockSpec((tokens, d), lambda i: (0, 1)),
            pl.BlockSpec((cb, d), lambda i: (i, 0)),
            pl.BlockSpec(memory_space=pltpu.HBM),
        ],
        out_specs=pl.BlockSpec((peers, 4, tokens), lambda i: (0, 0, 0)),
        out_shape=jax.ShapeDtypeStruct((peers, 4, tokens), F32),
        scratch_shapes=[pltpu.VMEM((8, tokens), F32)] * 3
        + [pltpu.VMEM((tokens, d), F32), pltpu.SemaphoreType.DMA],
        compiler_params=params(),
        cost_estimate=cost(4 * tokens * codes * d, codes * d * 2, tokens * codes),
        name="stats",
    )(toks, toks, book, rows)


def lat_step(sub, lat_ref, grad_ref, m_ref, book_ref, outs, weigh):
    count = book_ref.shape[0] // sub

    def block(j):
        return book_ref[j * sub : (j + 1) * sub, :]

    sums = [ref[...] for ref in outs]
    ahead = dot(lat_ref[...], block(0), NT)
    for j in range(count):
        logit = ahead
        if j + 1 < count:
            ahead = dot(lat_ref[...], block(j + 1), NT)
        back = dot(grad_ref[...], block(j), NT)
        terms = weigh(jnp.exp(logit - m_ref[:, :1]), back)
        sums = [x + dot(term.astype(BF16), block(j), NN) for x, term in zip(sums, terms)]
    for ref, x in zip(outs, sums):
        ref[...] = x


def first_kernel(sub, lat_ref, grad_ref, book_ref, pack_ref, a_ref, b_ref, m_ref, mean_ref):
    @pl.when(pl.program_id(0) == 0)
    def _():
        m_ref[...] = as_cols(pack_ref[0, 0:1, :])
        mean_ref[...] = as_cols(pack_ref[0, 2:3, :] / pack_ref[0, 1:2, :])
        a_ref[...] = jnp.zeros_like(a_ref)
        b_ref[...] = jnp.zeros_like(b_ref)

    def weigh(expo, back):
        return expo * (back - mean_ref[:, :1]), expo

    lat_step(sub, lat_ref, grad_ref, m_ref, book_ref, (a_ref, b_ref), weigh)


def second_kernel(
    steps, sub, lat_ref, grad_ref, book_ref, pack_ref, all_ref, a_hbm, b_hbm, rows_hbm,
    part_ref, sum_ref, lse_col, mean_col, a_ref, b_ref, rows_ref, sem,
):
    i = pl.program_id(0)
    pairs = ((a_hbm, a_ref), (b_hbm, b_ref), (rows_hbm, rows_ref))
    loads = [pltpu.make_async_copy(src, dst, sem.at[n]) for n, (src, dst) in enumerate(pairs)]

    @pl.when(i == 0)
    def _():
        for load in loads:
            load.start()
        lse_col[...] = as_cols(all_ref[0, 0:1, :])
        mean_col[...] = as_cols(all_ref[0, 1:2, :])
        sum_ref[...] = jnp.zeros_like(sum_ref)

    def weigh(prob, back):
        return (prob * (back - mean_col[:, :1]) + ce_weight * prob,)

    lat_step(sub, lat_ref, grad_ref, lse_col, book_ref, (sum_ref,), weigh)

    @pl.when(i == steps - 1)
    def _():
        for load in loads:
            load.wait()
        own = jnp.exp(pack_ref[0, 0:1, :] - all_ref[0, 0:1, :])
        local = pack_ref[0, 2:3, :] / pack_ref[0, 1:2, :]
        ratio = own * (ce_weight + local - all_ref[0, 1:2, :])
        part = as_cols(own)[:, :1] * a_ref[...] + as_cols(ratio)[:, :1] * b_ref[...]
        part_ref[...] = (sum_ref[...] + part - ce_weight * rows_ref[...]).astype(part_ref.dtype)


def lat_specs(tokens, d, cb, first):
    return [
        pl.BlockSpec((tokens, d), lambda i: (0, 0)),
        pl.BlockSpec((tokens, d), lambda i: (0, 1)),
        pl.BlockSpec((cb, d), lambda i: (i + first, 0)),
        pl.BlockSpec((1, 4, tokens), lambda i: (0, 0, 0)),
    ]


def lat_first(toks, packed, book, part=1, parts=2, cb=2048, sub=512):
    tokens, (codes, d) = toks.shape[0], book.shape
    steps = codes // cb * part // parts
    whole = pl.BlockSpec((tokens, d), lambda i: (0, 0))
    return pl.pallas_call(
        functools.partial(first_kernel, sub),
        grid=(steps,),
        in_specs=lat_specs(tokens, d, cb, 0),
        out_specs=[whole] * 2,
        out_shape=[pltpu.HBM((tokens, d), F32)] * 2,
        scratch_shapes=[pltpu.VMEM((tokens, 128), F32)] * 2,
        compiler_params=params(),
        cost_estimate=cost(8 * tokens * cb * steps * d, cb * steps * d * 2, tokens * cb * steps),
        name="lat_first",
    )(toks, toks, book, packed)


def lat_second(toks, packed, book, a, b, rows, row, part=1, parts=2, cb=4096, sub=512):
    tokens, (codes, d) = toks.shape[0], book.shape
    first = codes // cb * part // parts
    steps = codes // cb - first
    whole = pl.BlockSpec((tokens, d), lambda i: (0, 0))
    return pl.pallas_call(
        functools.partial(second_kernel, steps, sub),
        grid=(steps,),
        in_specs=lat_specs(tokens, d, cb, first)
        + [pl.BlockSpec((1, 4, tokens), lambda i: (0, 0, 0))]
        + [pl.BlockSpec(memory_space=pltpu.HBM)] * 3,
        out_specs=whole,
        out_shape=jax.ShapeDtypeStruct((tokens, d), BF16),
        scratch_shapes=[pltpu.VMEM((tokens, d), F32)]
        + [pltpu.VMEM((tokens, 128), F32)] * 2
        + [pltpu.VMEM((tokens, d), F32)] * 3
        + [pltpu.SemaphoreType.DMA((3,))],
        compiler_params=params(),
        cost_estimate=cost(6 * tokens * cb * steps * d, cb * steps * d * 2, tokens * cb * steps),
        name="lat_second",
    )(toks, toks, book, packed, row, a, b, rows)


def combine_kernel(all_ref, tgt_ref, first_ref, row_ref, loss_ref):
    stats = all_ref[...]
    m, l, w = stats[:, 0, :], stats[:, 1, :], stats[:, 2, :]
    tokens = m.shape[1]
    top = jnp.max(m, axis=0, keepdims=True)
    scale = jnp.exp(m - top)
    total = jnp.sum(l * scale, axis=0, keepdims=True)
    mean = jnp.sum(w * scale, axis=0, keepdims=True) / total
    lse = top + jnp.log(total)
    pack = jnp.concatenate([lse, mean, tgt_ref[...].astype(F32), mean], axis=0)
    row_ref[...] = jnp.broadcast_to(pack[None], row_ref.shape)
    loss = jnp.broadcast_to(lse - jnp.sum(stats[:, 3, :], axis=0, keepdims=True), (8, tokens))
    loss_ref[...] = pltpu.roll(loss, first_ref[0], 1)[:1, : loss_ref.shape[1]]


def combine(stats, tgt, first, groups, count):
    tokens = stats.shape[-1]
    vmem = pl.BlockSpec(memory_space=pltpu.VMEM)
    return pl.pallas_call(
        combine_kernel,
        in_specs=[vmem, vmem, pl.BlockSpec(memory_space=pltpu.SMEM)],
        out_shape=[
            jax.ShapeDtypeStruct((groups, 4, tokens), F32),
            jax.ShapeDtypeStruct((1, count), F32),
        ],
        compiler_params=params(),
        cost_estimate=cost(tokens * 1000, tokens * 800),
        name="combine",
    )(stats, tgt, first)


def book_kernel(sub, batch, s_ref, rows_ref, book_ref, *rest):
    groups = len(rest) - 3
    toks, (out_ref, buf, sem) = rest[:groups], rest[groups:]
    for g in range(groups):
        pltpu.make_async_copy(toks[g], buf.at[g], sem.at[g]).start()
    chunk, d = book_ref.shape
    tokens = buf.shape[1]
    ids = lax.broadcasted_iota(jnp.int32, (sub, tokens), 0) + s_ref[groups]
    out_ref[...] = jnp.zeros_like(out_ref)

    def block(j):
        return book_ref[j * sub : (j + 1) * sub, :]

    def step(i, carry):
        work = [(i * batch + k, j) for k in range(batch) for j in range(chunk // sub)]

        def logits(g, j):
            if j == 0:
                pltpu.make_async_copy(toks[0], buf.at[g], sem.at[g]).wait()
            return dot(block(j), buf[g, :, :d], NT)

        ahead = logits(*work[0])
        for n, (g, j) in enumerate(work):
            logit = ahead
            if n + 1 < len(work):
                ahead = logits(*work[n + 1])
            row = rows_ref[s_ref[g]]
            back = dot(block(j), buf[g, :, d:], NT)
            prob = jnp.exp(logit - row[0:1])
            hit = jnp.where(ids + j * sub == row[2:3].astype(jnp.int32), 1.0, 0.0)
            delta = prob * (back - row[1:2]) + ce_weight * (prob - hit)
            at = slice(j * sub, (j + 1) * sub)
            out_ref[at, :] += dot(delta.astype(BF16), buf[g, :, :d], NN) + dot(
                hit.astype(BF16), buf[g, :, d:], NN
            )
        return carry

    lax.fori_loop(0, groups // batch, step, 0)


def book_grad(scalars, rows, book, toks, sub=1024, batch=1):
    groups = len(toks)
    (tokens, width), (chunk, d) = toks[0].shape, book.shape
    whole = pl.BlockSpec((chunk, d), lambda i, s: (0, 0))
    grid_spec = pltpu.PrefetchScalarGridSpec(
        num_scalar_prefetch=1,
        grid=(1,),
        in_specs=[pl.BlockSpec(rows.shape, lambda i, s: (0, 0, 0)), whole]
        + [pl.BlockSpec(memory_space=pl.ANY)] * groups,
        out_specs=whole,
        scratch_shapes=[
            pltpu.VMEM((groups, tokens, width), BF16),
            pltpu.SemaphoreType.DMA((groups,)),
        ],
    )
    return pl.pallas_call(
        functools.partial(book_kernel, sub, batch),
        grid_spec=grid_spec,
        out_shape=jax.ShapeDtypeStruct((chunk, d), F32),
        compiler_params=params(),
        cost_estimate=cost(
            8 * groups * tokens * chunk * d, groups * tokens * width * 2, groups * tokens * chunk
        ),
        name="book_grad",
    )(scalars, rows, book, *toks)


def spread_kernel(lat_ref, grad_ref, out_ref):
    both = jnp.concatenate([lat_ref[...], grad_ref[...]], axis=1)
    out_ref[...] = jnp.broadcast_to(both[None], out_ref.shape)


def spread(lat, grad, peers):
    count, d = lat.shape
    return pl.pallas_call(
        spread_kernel,
        out_shape=jax.ShapeDtypeStruct((peers, count, 2 * d), BF16),
        compiler_params=params(),
        name="spread",
    )(lat, grad)


def gather_kernel(in_ref, out_ref):
    out_ref[...] = jnp.sum(in_ref[...].astype(F32), axis=0).astype(out_ref.dtype)


def sum_parts(parts):
    return pl.pallas_call(
        gather_kernel,
        out_shape=jax.ShapeDtypeStruct(parts.shape[1:], BF16),
        compiler_params=params(),
        name="sum_parts",
    )(parts)


def in_hbm(*arrays):
    return [pltpu.with_memory_space_constraint(x, pltpu.HBM) for x in arrays]


def per_device(latents, out_grad, targets, codebook):
    peers = lax.axis_size("z") * lax.axis_size("y")
    nx = lax.axis_size("x")
    own_count, d = latents.shape
    code_dev = codebook.shape[0]
    tokens = own_count * peers
    code_pos = lax.axis_index(ZY)
    x_pos, core = lax.axis_index("x"), lax.axis_index("core")
    dp_pos, chunk = x_pos * 2 + core, code_dev // (2 * nx)
    swap = [(0, 1), (1, 0)]
    book = pltpu.with_memory_space_constraint(codebook, pltpu.HBM)

    toks = lax.all_to_all(spread(*in_hbm(latents, out_grad), peers), ZY, 0, 0)
    toks = toks.reshape(tokens, 2 * d)
    local_ids = targets - code_pos * code_dev
    rows = pick_rows(jnp.broadcast_to(local_ids[:, None], (tokens, 128)), book)
    (rows,) = in_hbm(rows)
    places = [lax.rem(x_pos + nx - k, nx) * 2 for k in range(nx)]
    scalars = [p + core for p in places] + [p + 1 - core for p in places]
    scalars += [code_pos * code_dev + dp_pos * chunk]
    scalars = jnp.stack(scalars).astype(jnp.int32)
    own_book = lax.dynamic_slice(codebook, (dp_pos * chunk, 0), (chunk, d))
    packed = local_stats(toks, rows, book, peers)
    stats = lax.all_to_all(packed, ZY, 0, 0)
    same = [toks]
    for k in range(1, nx):
        same.append(lax.ppermute(toks, "x", [(i, (i + k) % nx) for i in range(nx)]))
    a, b = lat_first(toks, packed, book)
    shift = lax.rem(tokens - code_pos * own_count, tokens).astype(jnp.int32).reshape(1)
    row, loss = combine(stats, targets[None], shift, 2 * nx, own_count)
    everyone = lax.all_to_all(row, XC, 0, 0)
    part = lat_second(toks, packed, book, *in_hbm(a, b), rows, row)
    part, everyone = lax.optimization_barrier((part, everyone))
    moved = lax.all_to_all(part.reshape(peers, own_count, d), ZY, 0, 0)
    latent_grad = sum_parts(moved)
    token_loss = loss.reshape(own_count)

    other = []
    for piece in same:
        other.append(lax.ppermute(piece, "core", swap))
    codebook_grad = book_grad(scalars, everyone, own_book, same + other)
    return latent_grad, codebook_grad, token_loss


def solution(mesh):
    shape = (mesh.shape["dp"] // 2, 2, mesh.shape["code"] // 4, 4)
    fine = Mesh(mesh.devices.reshape(shape), ("x", "core", "z", "y"))
    dp, code = ("x", "core"), ("z", "y")
    in_specs = (P(dp + code, None), P(dp + code, None), P(dp), P(code, None))
    out_specs = (P(dp + code, None), P(code + dp, None), P(dp + code))
    return jax.shard_map(
        per_device, mesh=fine, in_specs=in_specs, out_specs=out_specs, check_vma=False
    )
```

profile of v0, /device:TPU:1, one launch (start us, length us, event | category | flops | bytes accessed | tf_op | source)
XLA Modules:
  0.0 96.2 jit_solution(234910550378516255)
XLA Ops:
  0.6 1.6 %spread.1 = bf16[32,16,512]{2,1,0:T(8,128)(2,1)} custom-call(bf16[16,256]{1,0:T(8,128)(2,1)} %lat_ref.1, bf16[16,256]{1,0:T(8,128)(2,1)} %grad_ref.1), custom_call_target="tpu_custom_call" | custom-call | tf_op jit(solution)/shard_map/spread/pallas_call | solution.py:364
  2.2 12.0 %all-to-all-start = ((bf16[32,16,512]{2,1,0:T(8,128)(2,1)}), bf16[32,16,512]{2,1,0:T(8,128)(2,1)S(1)}, u32[]{:S(2)}, u32[]{:S(2)}) async-start(bf16[32,16,512]{2,1,0:T(8,128)(2,1)} %spread.1), calls=%async_computation | async-start | bytes 1048576 | tf_op jit(solution)/shard_map/all_to_all | solution.py:401
  14.3 0.1 stack.39.s_ref
  14.3 0.7 broadcast_subtract_fusion
  15.0 0.1 broadcast_in_dim.4.tgt_ref
  15.2 5.7 %pick.1.rows_hbm = f32[512,256]{1,0:T(8,128)} custom-call(s32[512,128]{1,0:T(8,128)S(1)} %broadcast_in_dim.4.tgt_ref, bf16[8192,256]{1,0:T(8,128)(2,1)} %book_ref.7), custom_call_target="tpu_custom_call" | custom-call | flops 2147483648 | bytes 4194304 | tf_op jit(solution)/shard_map/pick/pallas_call | solution.py:49
  20.8 9.7 %all-to-all-done = bf16[32,16,512]{2,1,0:T(8,128)(2,1)S(1)} async-done(((bf16[32,16,512]{2,1,0:T(8,128)(2,1)}), bf16[32,16,512]{2,1,0:T(8,128)(2,1)S(1)}, u32[]{:S(2)}, u32[]{:S(2)}) %all-to-all-start) | async-done | bytes 524320 | tf_op jit(solution)/shard_map/all_to_all | solution.py:401
  30.5 1.2 %collective-permute-start = (bf16[512,512]{1,0:T(8,128)(2,1)S(1)}, bf16[512,512]{1,0:T(8,128)(2,1)S(1)}, u32[]{:S(2)}, u32[]{:S(2)}) collective-permute-start(bf16[512,512]{1,0:T(8,128)(2,1)S(1)} %bitcast.14), channel_id=1, source_target_pairs={{0,64},{64,128},{128,192},{192,0},{1,65},{65,129},{129,193},{193,1... | collective-permute-start | bytes 1572872 | tf_op jit(solution)/shard_map/ppermute | solution.py:415
  31.7 2.5 %collective-permute-start.1 = (bf16[512,512]{1,0:T(8,128)(2,1)S(1)}, bf16[512,512]{1,0:T(8,128)(2,1)S(1)}, u32[]{:S(2)}, u32[]{:S(2)}) collective-permute-start(bf16[512,512]{1,0:T(8,128)(2,1)S(1)} %bitcast.15), channel_id=1, source_target_pairs={{0,128},{64,192},{128,0},{192,64},{1,129},{65,193},{129,1},{193,65... | collective-permute-start | bytes 1572872 | tf_op jit(solution)/shard_map/ppermute | solution.py:415
  34.2 1.2 %collective-permute-start.2 = (bf16[512,512]{1,0:T(8,128)(2,1)S(1)}, bf16[512,512]{1,0:T(8,128)(2,1)S(1)}, u32[]{:S(2)}, u32[]{:S(2)}) collective-permute-start(bf16[512,512]{1,0:T(8,128)(2,1)S(1)} %bitcast.16), channel_id=1, source_target_pairs={{0,192},{64,0},{128,64},{192,128},{1,193},{65,1},{129,65},{193,129... | collective-permute-start | bytes 1572872 | tf_op jit(solution)/shard_map/ppermute | solution.py:415
  35.3 7.7 %stats.1.pack_ref = f32[32,4,512]{2,1,0:T(4,128)} custom-call(bf16[512,512]{1,0:T(8,128)(2,1)S(1)} %bitcast.17, bf16[512,512]{1,0:T(8,128)(2,1)S(1)} %bitcast.18, bf16[8192,256]{1,0:T(8,128)(2,1)} %book_ref.7, f32[512,256]{1,0:T(8,128)} %pick.1.rows_hbm), custom_call_target="tpu_custom_call" | custom-call | flops 4294967296 | bytes 4194304 | tf_op jit(solution)/shard_map/stats/pallas_call | solution.py:126
  43.0 5.3 %all-to-all-start.1 = ((f32[32,4,512]{2,1,0:T(4,128)}), f32[32,4,512]{2,1,0:T(4,128)S(1)}, u32[]{:S(2)}, u32[]{:S(2)}) async-start(f32[32,4,512]{2,1,0:T(4,128)} %stats.1.pack_ref), calls=%async_computation.1 | async-start | bytes 524288 | tf_op jit(solution)/shard_map/all_to_all | solution.py:412
  48.3 1.1 %constant_dynamic-slice_fusion.book_ref = bf16[1024,256]{1,0:T(8,128)(2,1)S(1)} fusion(bf16[8192,256]{1,0:T(8,128)(2,1)} %book_ref.7, s32[]{:T(128)S(6)} %select_n.3), kind=kLoop, calls=%fused_computation.1 | loop fusion | bytes 1048580 | tf_op jit(solution)/shard_map/dynamic_slice | solution.py:410
  49.4 2.7 %collective-permute-start.3 = (bf16[512,512]{1,0:T(8,128)(2,1)S(1)}, bf16[512,512]{1,0:T(8,128)(2,1)S(1)}, u32[]{:S(2)}, u32[]{:S(2)}) collective-permute-start(bf16[512,512]{1,0:T(8,128)(2,1)S(1)} %bitcast.19), channel_id=1, source_target_pairs={{0,32},{32,0},{1,33},{33,1},{2,34},{34,2},{3,35},{35,3},{4,36},{36... | collective-permute-start | bytes 1572872 | tf_op jit(solution)/shard_map/ppermute | solution.py:428
  52.1 0.1 collective-permute-start.4
  52.2 2.8 %collective-permute-done.1.rest_2_ = bf16[512,512]{1,0:T(8,128)(2,1)S(1)} collective-permute-done((bf16[512,512]{1,0:T(8,128)(2,1)S(1)}, bf16[512,512]{1,0:T(8,128)(2,1)S(1)}, u32[]{:S(2)}, u32[]{:S(2)}) %collective-permute-start.1) | collective-permute-done | bytes 524320 | tf_op jit(solution)/shard_map/ppermute | solution.py:415
  55.0 3.3 %collective-permute-start.5 = (bf16[512,512]{1,0:T(8,128)(2,1)S(1)}, bf16[512,512]{1,0:T(8,128)(2,1)}, u32[]{:S(2)}, u32[]{:S(2)}) collective-permute-start(bf16[512,512]{1,0:T(8,128)(2,1)S(1)} %collective-permute-done.1.rest_2_), channel_id=1, source_target_pairs={{0,32},{32,0},{1,33},{33,1},{2,34},{34,2},{3,35},{35,3},{4,36},{36... | collective-permute-start | bytes 1572872 | tf_op jit(solution)/shard_map/ppermute | solution.py:428
  58.3 7.3 %lat_first.1 = (f32[512,256]{1,0:T(8,128)}, f32[512,256]{1,0:T(8,128)}) custom-call(bf16[512,512]{1,0:T(8,128)(2,1)S(1)} %bitcast.20, bf16[512,512]{1,0:T(8,128)(2,1)S(1)} %bitcast.21, bf16[8192,256]{1,0:T(8,128)(2,1)} %book_ref.7, f32[32,4,512]{2,1,0:T(4,128)} %stats.1.pack_ref), custom_call_target="tpu_custom_call" | custom-call | flops 4294967296 | bytes 2097152 | tf_op jit(solution)/shard_map/lat_first/pallas_call | solution.py:223
  65.6 0.8 combine.1
  66.3 4.0 %all-to-all-start.2 = ((f32[8,4,512]{2,1,0:T(4,128)}), f32[8,4,512]{2,1,0:T(4,128)S(1)}, u32[]{:S(2)}, u32[]{:S(2)}) async-start(f32[8,4,512]{2,1,0:T(4,128)} %get-tuple-element.9.all_ref), calls=%async_computation.2 | async-start | bytes 131072 | tf_op jit(solution)/shard_map/all_to_all | solution.py:419
  70.4 6.4 %lat_second.1 = bf16[512,256]{1,0:T(8,128)(2,1)} custom-call(bf16[512,512]{1,0:T(8,128)(2,1)S(1)} %bitcast.22, bf16[512,512]{1,0:T(8,128)(2,1)S(1)} %bitcast.23, bf16[8192,256]{1,0:T(8,128)(2,1)} %book_ref.7, f32[32,4,512]{2,1,0:T(4,128)} %stats.1.pack_ref, f32[8,4,512]{2,1,0:T(4,128)} %get-tuple-element.9.all_ref, f32[512,256]{1,0:T(8,128)} %get-tuple-element.10.a_hbm, ...), custom_call_target="tpu_custom_call" | custom-call | flops 3221225472 | bytes 2097152 | tf_op jit(solution)/shard_map/lat_second/pallas_call | solution.py:241
  76.8 5.3 %all-to-all-start.3 = ((bf16[32,16,256]{2,1,0:T(8,128)(2,1)}), bf16[32,16,256]{2,1,0:T(8,128)(2,1)S(1)}, u32[]{:S(2)}, u32[]{:S(2)}) async-start(bf16[32,16,256]{2,1,0:T(8,128)(2,1)} %bitcast.3), calls=%async_computation.3 | async-start | bytes 524288 | tf_op jit(solution)/shard_map/all_to_all | solution.py:422
  82.1 13.4 %book_grad.1 = f32[1024,256]{1,0:T(8,128)} custom-call(s32[9]{0:T(128)S(1)} %stack.39.s_ref, f32[8,4,512]{2,1,0:T(4,128)S(1)} %all-to-all-done.2.rows_ref, bf16[1024,256]{1,0:T(8,128)(2,1)S(1)} %constant_dynamic-slice_fusion.book_ref, bf16[512,512]{1,0:T(8,128)(2,1)S(1)} %bitcast.24, bf16[512,512]{1,0:T(8,128)(2,1)S(1)} %collective-permute-done.rest_1_, ...), custom_call_target="tpu_custom_call" | custom-call | flops 8589934592 | bytes 4194304 | tf_op jit(solution)/shard_map/book_grad/pallas_call | solution.py:345
  95.5 0.6 sum_parts.1
  (12 shorter events, 0.0 us)
Async XLA Ops:
  2.2 28.3 %all-to-all-start = ((bf16[32,16,512]{2,1,0:T(8,128)(2,1)}), bf16[32,16,512]{2,1,0:T(8,128)(2,1)S(1)}, u32[]{:S(2)}, u32[]{:S(2)}) async-start(bf16[32,16,512]{2,1,0:T(8,128)(2,1)} %spread.1), calls=%async_computation | async-start | bytes 1048576 | tf_op jit(solution)/shard_map/all_to_all | solution.py:401
  30.5 21.6 %collective-permute-start = (bf16[512,512]{1,0:T(8,128)(2,1)S(1)}, bf16[512,512]{1,0:T(8,128)(2,1)S(1)}, u32[]{:S(2)}, u32[]{:S(2)}) collective-permute-start(bf16[512,512]{1,0:T(8,128)(2,1)S(1)} %bitcast.14), channel_id=1, source_target_pairs={{0,64},{64,128},{128,192},{192,0},{1,65},{65,129},{129,193},{193,1... | collective-permute-start | bytes 1572872 | tf_op jit(solution)/shard_map/ppermute | solution.py:415
  31.7 23.3 %collective-permute-start.1 = (bf16[512,512]{1,0:T(8,128)(2,1)S(1)}, bf16[512,512]{1,0:T(8,128)(2,1)S(1)}, u32[]{:S(2)}, u32[]{:S(2)}) collective-permute-start(bf16[512,512]{1,0:T(8,128)(2,1)S(1)} %bitcast.15), channel_id=1, source_target_pairs={{0,128},{64,192},{128,0},{192,64},{1,129},{65,193},{129,1},{193,65... | collective-permute-start | bytes 1572872 | tf_op jit(solution)/shard_map/ppermute | solution.py:415
  34.2 24.1 %collective-permute-start.2 = (bf16[512,512]{1,0:T(8,128)(2,1)S(1)}, bf16[512,512]{1,0:T(8,128)(2,1)S(1)}, u32[]{:S(2)}, u32[]{:S(2)}) collective-permute-start(bf16[512,512]{1,0:T(8,128)(2,1)S(1)} %bitcast.16), channel_id=1, source_target_pairs={{0,192},{64,0},{128,64},{192,128},{1,193},{65,1},{129,65},{193,129... | collective-permute-start | bytes 1572872 | tf_op jit(solution)/shard_map/ppermute | solution.py:415
  43.0 22.6 %all-to-all-start.1 = ((f32[32,4,512]{2,1,0:T(4,128)}), f32[32,4,512]{2,1,0:T(4,128)S(1)}, u32[]{:S(2)}, u32[]{:S(2)}) async-start(f32[32,4,512]{2,1,0:T(4,128)} %stats.1.pack_ref), calls=%async_computation.1 | async-start | bytes 524288 | tf_op jit(solution)/shard_map/all_to_all | solution.py:412
  49.4 16.2 %copy-start = (s32[512]{0:T(512)S(1)}, s32[512]{0:T(512)}, u32[]{:S(2)}) copy-start(s32[512]{0:T(512)} %param.6) | copy-start | bytes 6148
  49.4 32.7 %collective-permute-start.3 = (bf16[512,512]{1,0:T(8,128)(2,1)S(1)}, bf16[512,512]{1,0:T(8,128)(2,1)S(1)}, u32[]{:S(2)}, u32[]{:S(2)}) collective-permute-start(bf16[512,512]{1,0:T(8,128)(2,1)S(1)} %bitcast.19), channel_id=1, source_target_pairs={{0,32},{32,0},{1,33},{33,1},{2,34},{34,2},{3,35},{35,3},{4,36},{36... | collective-permute-start | bytes 1572872 | tf_op jit(solution)/shard_map/ppermute | solution.py:428
  52.1 29.9 %collective-permute-start.4 = (bf16[512,512]{1,0:T(8,128)(2,1)S(1)}, bf16[512,512]{1,0:T(8,128)(2,1)}, u32[]{:S(2)}, u32[]{:S(2)}) collective-permute-start(bf16[512,512]{1,0:T(8,128)(2,1)S(1)} %collective-permute-done.rest_1_), channel_id=1, source_target_pairs={{0,32},{32,0},{1,33},{33,1},{2,34},{34,2},{3,35},{35,3},{4,36},{36... | collective-permute-start | bytes 1572872 | tf_op jit(solution)/shard_map/ppermute | solution.py:428
  55.0 27.1 %collective-permute-start.5 = (bf16[512,512]{1,0:T(8,128)(2,1)S(1)}, bf16[512,512]{1,0:T(8,128)(2,1)}, u32[]{:S(2)}, u32[]{:S(2)}) collective-permute-start(bf16[512,512]{1,0:T(8,128)(2,1)S(1)} %collective-permute-done.1.rest_2_), channel_id=1, source_target_pairs={{0,32},{32,0},{1,33},{33,1},{2,34},{34,2},{3,35},{35,3},{4,36},{36... | collective-permute-start | bytes 1572872 | tf_op jit(solution)/shard_map/ppermute | solution.py:428
  58.3 23.8 %collective-permute-start.6 = (bf16[512,512]{1,0:T(8,128)(2,1)S(1)}, bf16[512,512]{1,0:T(8,128)(2,1)}, u32[]{:S(2)}, u32[]{:S(2)}) collective-permute-start(bf16[512,512]{1,0:T(8,128)(2,1)S(1)} %collective-permute-done.2.rest_3_), channel_id=1, source_target_pairs={{0,32},{32,0},{1,33},{33,1},{2,34},{34,2},{3,35},{35,3},{4,36},{36... | collective-permute-start | bytes 1572872 | tf_op jit(solution)/shard_map/ppermute | solution.py:428
  66.3 10.4 %all-to-all-start.2 = ((f32[8,4,512]{2,1,0:T(4,128)}), f32[8,4,512]{2,1,0:T(4,128)S(1)}, u32[]{:S(2)}, u32[]{:S(2)}) async-start(f32[8,4,512]{2,1,0:T(4,128)} %get-tuple-element.9.all_ref), calls=%async_computation.2 | async-start | bytes 131072 | tf_op jit(solution)/shard_map/all_to_all | solution.py:419
  76.8 18.7 %all-to-all-start.3 = ((bf16[32,16,256]{2,1,0:T(8,128)(2,1)}), bf16[32,16,256]{2,1,0:T(8,128)(2,1)S(1)}, u32[]{:S(2)}, u32[]{:S(2)}) async-start(bf16[32,16,256]{2,1,0:T(8,128)(2,1)} %bitcast.3), calls=%async_computation.3 | async-start | bytes 524288 | tf_op jit(solution)/shard_map/all_to_all | solution.py:422
where the time goes:
time: 96.8 us; the launch traced here: 96.2 us
  Pallas kernels  43.4 us (45%)
  starting transfers between devices  37.5 us (39%)
  waiting for transfers between devices  12.5 us (13%)
  local copies, waits for them, and re-layouts  1.3 us (1%)
    pallas_call x1, Pallas kernels, book_grad(): pl.pallas_call(functools.partial(book_kernel, sub, batch), grid_spec=grid...  13.4 us
    all_to_all x1, starting transfers between devices, per_device(): toks = lax.all_to_all(spread(*in_hbm(latents, out_grad), peers), ZY, 0, 0)  12 us
    all_to_all x1, waiting for transfers between devices, per_device(): toks = lax.all_to_all(spread(*in_hbm(latents, out_grad), peers), ZY, 0, 0)  9.68 us
    pallas_call x1, Pallas kernels, local_stats(): pl.pallas_call(functools.partial(stats_kernel, steps, sub), grid=(steps,)...  7.67 us
    pallas_call x1, Pallas kernels, lat_first(): pl.pallas_call(functools.partial(first_kernel, sub), grid=(steps,), in_sp...  7.27 us
    pallas_call x1, Pallas kernels, lat_second(): pl.pallas_call(functools.partial(second_kernel, steps, sub), grid=(steps,...  6.37 us
    ppermute x4, starting transfers between devices, per_device(): other.append(lax.ppermute(piece, 'core', swap))  6.14 us
    pallas_call x1, Pallas kernels, pick_rows(): pl.pallas_call(functools.partial(pick_kernel, cb), grid=(codes // cb,), i...  5.67 us
  transfers between devices with their start and end apart: 11, of which 2 were waited for; matrix products, arithmetic and copies ran while one was open for 2% of the time, Pallas kernels for 43%

commit v1 on v0

--- a/solution.py
+++ b/solution.py
@@ -176,35 +176,32 @@
 
 
 def second_kernel(
-    steps, sub, lat_ref, grad_ref, book_ref, pack_ref, all_ref, a_hbm, b_hbm, rows_hbm,
-    part_ref, sum_ref, lse_col, mean_col, a_ref, b_ref, rows_ref, sem,
+    first, sub, lat_ref, grad_ref, pack_ref, all_ref, book_hbm, a_hbm, b_hbm, rows_hbm,
+    part_ref, sum_ref, lse_col, mean_col, book_ref, a_ref, b_ref, rows_ref, sem,
 ):
-    i = pl.program_id(0)
+    near = pltpu.make_async_copy(book_hbm.at[pl.ds(first, book_ref.shape[0])], book_ref, sem.at[3])
+    near.start()
     pairs = ((a_hbm, a_ref), (b_hbm, b_ref), (rows_hbm, rows_ref))
     loads = [pltpu.make_async_copy(src, dst, sem.at[n]) for n, (src, dst) in enumerate(pairs)]
 
-    @pl.when(i == 0)
-    def _():
-        for load in loads:
-            load.start()
-        lse_col[...] = as_cols(all_ref[0, 0:1, :])
-        mean_col[...] = as_cols(all_ref[0, 1:2, :])
-        sum_ref[...] = jnp.zeros_like(sum_ref)
+    for load in loads:
+        load.start()
+    lse_col[...] = as_cols(all_ref[0, 0:1, :])
+    mean_col[...] = as_cols(all_ref[0, 1:2, :])
+    sum_ref[...] = jnp.zeros_like(sum_ref)
+    near.wait()
 
     def weigh(prob, back):
         return (prob * (back - mean_col[:, :1]) + ce_weight * prob,)
 
     lat_step(sub, lat_ref, grad_ref, lse_col, book_ref, (sum_ref,), weigh)
-
-    @pl.when(i == steps - 1)
-    def _():
-        for load in loads:
-            load.wait()
-        own = jnp.exp(pack_ref[0, 0:1, :] - all_ref[0, 0:1, :])
-        local = pack_ref[0, 2:3, :] / pack_ref[0, 1:2, :]
-        ratio = own * (ce_weight + local - all_ref[0, 1:2, :])
-        part = as_cols(own)[:, :1] * a_ref[...] + as_cols(ratio)[:, :1] * b_ref[...]
-        part_ref[...] = (sum_ref[...] + part - ce_weight * rows_ref[...]).astype(part_ref.dtype)
+    for load in loads:
+        load.wait()
+    own = jnp.exp(pack_ref[0, 0:1, :] - all_ref[0, 0:1, :])
+    local = pack_ref[0, 2:3, :] / pack_ref[0, 1:2, :]
+    ratio = own * (ce_weight + local - all_ref[0, 1:2, :])
+    part = as_cols(own)[:, :1] * a_ref[...] + as_cols(ratio)[:, :1] * b_ref[...]
+    part_ref[...] = (sum_ref[...] + part - ce_weight * rows_ref[...]).astype(part_ref.dtype)
 
 
 def lat_specs(tokens, d, cb, first):
@@ -216,9 +213,9 @@
     ]
 
 
-def lat_first(toks, packed, book, part=1, parts=2, cb=2048, sub=512):
+def lat_first(toks, packed, book, sub=512):
     tokens, (codes, d) = toks.shape[0], book.shape
-    steps = codes // cb * part // parts
+    steps, cb = 2, codes * 5 // 16
     whole = pl.BlockSpec((tokens, d), lambda i: (0, 0))
     return pl.pallas_call(
         functools.partial(first_kernel, sub),
@@ -233,27 +230,31 @@
     )(toks, toks, book, packed)
 
 
-def lat_second(toks, packed, book, a, b, rows, row, part=1, parts=2, cb=4096, sub=512):
+def lat_second(toks, packed, book, a, b, rows, row, sub=512):
     tokens, (codes, d) = toks.shape[0], book.shape
-    first = codes // cb * part // parts
-    steps = codes // cb - first
+    first = codes * 5 // 8
+    count = codes - first
     whole = pl.BlockSpec((tokens, d), lambda i: (0, 0))
     return pl.pallas_call(
-        functools.partial(second_kernel, steps, sub),
-        grid=(steps,),
-        in_specs=lat_specs(tokens, d, cb, first)
-        + [pl.BlockSpec((1, 4, tokens), lambda i: (0, 0, 0))]
-        + [pl.BlockSpec(memory_space=pltpu.HBM)] * 3,
+        functools.partial(second_kernel, first, sub),
+        grid=(1,),
+        in_specs=[
+            pl.BlockSpec((tokens, d), lambda i: (0, 0)),
+            pl.BlockSpec((tokens, d), lambda i: (0, 1)),
+        ]
+        + [pl.BlockSpec((1, 4, tokens), lambda i: (0, 0, 0))] * 2
+        + [pl.BlockSpec(memory_space=pltpu.HBM)] * 4,
         out_specs=whole,
         out_shape=jax.ShapeDtypeStruct((tokens, d), BF16),
         scratch_shapes=[pltpu.VMEM((tokens, d), F32)]
         + [pltpu.VMEM((tokens, 128), F32)] * 2
+        + [pltpu.VMEM((count, d), BF16)]
         + [pltpu.VMEM((tokens, d), F32)] * 3
-        + [pltpu.SemaphoreType.DMA((3,))],
-        compiler_params=params(),
-        cost_estimate=cost(6 * tokens * cb * steps * d, cb * steps * d * 2, tokens * cb * steps),
+        + [pltpu.SemaphoreType.DMA((4,))],
+        compiler_params=params(),
+        cost_estimate=cost(6 * tokens * count * d, count * d * 2, tokens * count),
         name="lat_second",
-    )(toks, toks, book, packed, row, a, b, rows)
+    )(toks, toks, packed, row, book, a, b, rows)
 
 
 def combine_kernel(all_ref, tgt_ref, first_ref, row_ref, loss_ref):

time: 96.8 us -> 97.6 us (level)
    pallas_call x1, Pallas kernels: 7.27 us -> 8.47 us  [lat_first(): pl.pallas_call(functools.partial(first_kernel, sub), grid=(steps,), in_sp...]
where the time goes in v1:
time: 97.6 us; the launch traced here: 96.8 us
  Pallas kernels  44 us (45%)
  starting transfers between devices  37.5 us (38%)
  waiting for transfers between devices  12.5 us (13%)
  local copies, waits for them, and re-layouts  1.3 us (1%)
    pallas_call x1, Pallas kernels, book_grad(): pl.pallas_call(functools.partial(book_kernel, sub, batch), grid_spec=grid...  13.2 us
    all_to_all x1, starting transfers between devices, per_device(): toks = lax.all_to_all(spread(*in_hbm(latents, out_grad), peers), ZY, 0, 0)  12 us
    all_to_all x1, waiting for transfers between devices, per_device(): toks = lax.all_to_all(spread(*in_hbm(latents, out_grad), peers), ZY, 0, 0)  9.82 us
    pallas_call x1, Pallas kernels, lat_first(): pl.pallas_call(functools.partial(first_kernel, sub), grid=(steps,), in_sp...  8.47 us
    pallas_call x1, Pallas kernels, local_stats(): pl.pallas_call(functools.partial(stats_kernel, steps, sub), grid=(steps,)...  7.67 us
    ppermute x4, starting transfers between devices, per_device(): other.append(lax.ppermute(piece, 'core', swap))  6.13 us
    pallas_call x1, Pallas kernels, lat_second(): pl.pallas_call(functools.partial(second_kernel, first, sub), grid=(1,), i...  6.04 us
    pallas_call x1, Pallas kernels, pick_rows(): pl.pallas_call(functools.partial(pick_kernel, cb), grid=(codes // cb,), i...  5.64 us
  transfers between devices with their start and end apart: 11, of which 2 were waited for; matrix products, arithmetic and copies ran while one was open for 2% of the time, Pallas kernels for 43%

profile of v1, /device:TPU:1, one launch (start us, length us, event | category | flops | bytes accessed | tf_op | source)
XLA Modules:
  0.0 96.8 jit_solution(17476586691808793148)
XLA Ops:
  0.6 1.6 %spread.1 = bf16[32,16,512]{2,1,0:T(8,128)(2,1)} custom-call(bf16[16,256]{1,0:T(8,128)(2,1)} %lat_ref.1, bf16[16,256]{1,0:T(8,128)(2,1)} %grad_ref.1), custom_call_target="tpu_custom_call" | custom-call | tf_op jit(solution)/shard_map/spread/pallas_call | solution.py:365
  2.2 12.0 %all-to-all-start = ((bf16[32,16,512]{2,1,0:T(8,128)(2,1)}), bf16[32,16,512]{2,1,0:T(8,128)(2,1)S(1)}, u32[]{:S(2)}, u32[]{:S(2)}) async-start(bf16[32,16,512]{2,1,0:T(8,128)(2,1)} %spread.1), calls=%async_computation | async-start | bytes 1048576 | tf_op jit(solution)/shard_map/all_to_all | solution.py:402
  14.2 0.7 broadcast_subtract_fusion
  14.9 0.1 broadcast_in_dim.4.tgt_ref
  15.1 5.6 %pick.1.rows_hbm = f32[512,256]{1,0:T(8,128)} custom-call(s32[512,128]{1,0:T(8,128)S(1)} %broadcast_in_dim.4.tgt_ref, bf16[8192,256]{1,0:T(8,128)(2,1)} %book_hbm.1), custom_call_target="tpu_custom_call" | custom-call | flops 2147483648 | bytes 4194304 | tf_op jit(solution)/shard_map/pick/pallas_call | solution.py:49
  20.7 9.8 %all-to-all-done = bf16[32,16,512]{2,1,0:T(8,128)(2,1)S(1)} async-done(((bf16[32,16,512]{2,1,0:T(8,128)(2,1)}), bf16[32,16,512]{2,1,0:T(8,128)(2,1)S(1)}, u32[]{:S(2)}, u32[]{:S(2)}) %all-to-all-start) | async-done | bytes 524320 | tf_op jit(solution)/shard_map/all_to_all | solution.py:402
  30.5 1.2 %collective-permute-start = (bf16[512,512]{1,0:T(8,128)(2,1)S(1)}, bf16[512,512]{1,0:T(8,128)(2,1)S(1)}, u32[]{:S(2)}, u32[]{:S(2)}) collective-permute-start(bf16[512,512]{1,0:T(8,128)(2,1)S(1)} %bitcast.14), channel_id=1, source_target_pairs={{0,64},{64,128},{128,192},{192,0},{1,65},{65,129},{129,193},{193,1... | collective-permute-start | bytes 1572872 | tf_op jit(solution)/shard_map/ppermute | solution.py:416
  31.7 2.5 %collective-permute-start.1 = (bf16[512,512]{1,0:T(8,128)(2,1)S(1)}, bf16[512,512]{1,0:T(8,128)(2,1)S(1)}, u32[]{:S(2)}, u32[]{:S(2)}) collective-permute-start(bf16[512,512]{1,0:T(8,128)(2,1)S(1)} %bitcast.15), channel_id=1, source_target_pairs={{0,128},{64,192},{128,0},{192,64},{1,129},{65,193},{129,1},{193,65... | collective-permute-start | bytes 1572872 | tf_op jit(solution)/shard_map/ppermute | solution.py:416
  34.2 1.2 %collective-permute-start.2 = (bf16[512,512]{1,0:T(8,128)(2,1)S(1)}, bf16[512,512]{1,0:T(8,128)(2,1)S(1)}, u32[]{:S(2)}, u32[]{:S(2)}) collective-permute-start(bf16[512,512]{1,0:T(8,128)(2,1)S(1)} %bitcast.16), channel_id=1, source_target_pairs={{0,192},{64,0},{128,64},{192,128},{1,193},{65,1},{129,65},{193,129... | collective-permute-start | bytes 1572872 | tf_op jit(solution)/shard_map/ppermute | solution.py:416
  35.3 7.7 %stats.1.pack_ref = f32[32,4,512]{2,1,0:T(4,128)} custom-call(bf16[512,512]{1,0:T(8,128)(2,1)S(1)} %bitcast.17, bf16[512,512]{1,0:T(8,128)(2,1)S(1)} %bitcast.18, bf16[8192,256]{1,0:T(8,128)(2,1)} %book_hbm.1, f32[512,256]{1,0:T(8,128)} %pick.1.rows_hbm), custom_call_target="tpu_custom_call" | custom-call | flops 4294967296 | bytes 4194304 | tf_op jit(solution)/shard_map/stats/pallas_call | solution.py:126
  43.0 5.3 %all-to-all-start.1 = ((f32[32,4,512]{2,1,0:T(4,128)}), f32[32,4,512]{2,1,0:T(4,128)S(1)}, u32[]{:S(2)}, u32[]{:S(2)}) async-start(f32[32,4,512]{2,1,0:T(4,128)} %stats.1.pack_ref), calls=%async_computation.1 | async-start | bytes 524288 | tf_op jit(solution)/shard_map/all_to_all | solution.py:413
  48.3 1.1 %constant_dynamic-slice_fusion.book_ref = bf16[1024,256]{1,0:T(8,128)(2,1)S(1)} fusion(bf16[8192,256]{1,0:T(8,128)(2,1)} %book_hbm.1, s32[]{:T(128)S(6)} %select_n.3), kind=kLoop, calls=%fused_computation.1 | loop fusion | bytes 1048580 | tf_op jit(solution)/shard_map/dynamic_slice | solution.py:411
  49.4 0.1 stack.39.s_ref
  49.5 2.7 %collective-permute-start.3 = (bf16[512,512]{1,0:T(8,128)(2,1)S(1)}, bf16[512,512]{1,0:T(8,128)(2,1)S(1)}, u32[]{:S(2)}, u32[]{:S(2)}) collective-permute-start(bf16[512,512]{1,0:T(8,128)(2,1)S(1)} %bitcast.19), channel_id=1, source_target_pairs={{0,32},{32,0},{1,33},{33,1},{2,34},{34,2},{3,35},{35,3},{4,36},{36... | collective-permute-start | bytes 1572872 | tf_op jit(solution)/shard_map/ppermute | solution.py:429
  52.2 0.1 collective-permute-start.4
  52.3 2.7 %collective-permute-done.1.rest_2_ = bf16[512,512]{1,0:T(8,128)(2,1)S(1)} collective-permute-done((bf16[512,512]{1,0:T(8,128)(2,1)S(1)}, bf16[512,512]{1,0:T(8,128)(2,1)S(1)}, u32[]{:S(2)}, u32[]{:S(2)}) %collective-permute-start.1) | collective-permute-done | bytes 524320 | tf_op jit(solution)/shard_map/ppermute | solution.py:416
  55.0 3.3 %collective-permute-start.5 = (bf16[512,512]{1,0:T(8,128)(2,1)S(1)}, bf16[512,512]{1,0:T(8,128)(2,1)}, u32[]{:S(2)}, u32[]{:S(2)}) collective-permute-start(bf16[512,512]{1,0:T(8,128)(2,1)S(1)} %collective-permute-done.1.rest_2_), channel_id=1, source_target_pairs={{0,32},{32,0},{1,33},{33,1},{2,34},{34,2},{3,35},{35,3},{4,36},{36... | collective-permute-start | bytes 1572872 | tf_op jit(solution)/shard_map/ppermute | solution.py:429
  58.3 8.5 %lat_first.1 = (f32[512,256]{1,0:T(8,128)}, f32[512,256]{1,0:T(8,128)}) custom-call(bf16[512,512]{1,0:T(8,128)(2,1)S(1)} %bitcast.20, bf16[512,512]{1,0:T(8,128)(2,1)S(1)} %bitcast.21, bf16[8192,256]{1,0:T(8,128)(2,1)} %book_hbm.1, f32[32,4,512]{2,1,0:T(4,128)} %stats.1.pack_ref), custom_call_target="tpu_custom_call" | custom-call | flops 5368709120 | bytes 2621440 | tf_op jit(solution)/shard_map/lat_first/pallas_call | solution.py:220
  66.8 0.8 combine.1
  67.5 4.0 %all-to-all-start.2 = ((f32[8,4,512]{2,1,0:T(4,128)}), f32[8,4,512]{2,1,0:T(4,128)S(1)}, u32[]{:S(2)}, u32[]{:S(2)}) async-start(f32[8,4,512]{2,1,0:T(4,128)} %get-tuple-element.9.all_ref), calls=%async_computation.2 | async-start | bytes 131072 | tf_op jit(solution)/shard_map/all_to_all | solution.py:420
  71.6 6.0 %lat_second.1 = bf16[512,256]{1,0:T(8,128)(2,1)} custom-call(bf16[512,512]{1,0:T(8,128)(2,1)S(1)} %bitcast.22, bf16[512,512]{1,0:T(8,128)(2,1)S(1)} %bitcast.23, f32[32,4,512]{2,1,0:T(4,128)} %stats.1.pack_ref, f32[8,4,512]{2,1,0:T(4,128)} %get-tuple-element.9.all_ref, bf16[8192,256]{1,0:T(8,128)(2,1)} %book_hbm.1, f32[512,256]{1,0:T(8,128)} %get-tuple-element.10.a_hbm, ...), custom_call_target="tpu_custom_call" | custom-call | flops 2415919104 | bytes 1572864 | tf_op jit(solution)/shard_map/lat_second/pallas_call | solution.py:238
  77.6 5.3 %all-to-all-start.3 = ((bf16[32,16,256]{2,1,0:T(8,128)(2,1)}), bf16[32,16,256]{2,1,0:T(8,128)(2,1)S(1)}, u32[]{:S(2)}, u32[]{:S(2)}) async-start(bf16[32,16,256]{2,1,0:T(8,128)(2,1)} %bitcast.3), calls=%async_computation.3 | async-start | bytes 524288 | tf_op jit(solution)/shard_map/all_to_all | solution.py:423
  83.0 13.2 %book_grad.1 = f32[1024,256]{1,0:T(8,128)} custom-call(s32[9]{0:T(128)S(1)} %stack.39.s_ref, f32[8,4,512]{2,1,0:T(4,128)S(1)} %all-to-all-done.2.rows_ref, bf16[1024,256]{1,0:T(8,128)(2,1)S(1)} %constant_dynamic-slice_fusion.book_ref, bf16[512,512]{1,0:T(8,128)(2,1)S(1)} %bitcast.24, bf16[512,512]{1,0:T(8,128)(2,1)S(1)} %collective-permute-done.rest_1_, ...), custom_call_target="tpu_custom_call" | custom-call | flops 8589934592 | bytes 4194304 | tf_op jit(solution)/shard_map/book_grad/pallas_call | solution.py:346
  96.1 0.6 sum_parts.1
  (12 shorter events, 0.0 us)
Async XLA Ops:
  2.2 28.3 %all-to-all-start = ((bf16[32,16,512]{2,1,0:T(8,128)(2,1)}), bf16[32,16,512]{2,1,0:T(8,128)(2,1)S(1)}, u32[]{:S(2)}, u32[]{:S(2)}) async-start(bf16[32,16,512]{2,1,0:T(8,128)(2,1)} %spread.1), calls=%async_computation | async-start | bytes 1048576 | tf_op jit(solution)/shard_map/all_to_all | solution.py:402
  30.5 21.7 %collective-permute-start = (bf16[512,512]{1,0:T(8,128)(2,1)S(1)}, bf16[512,512]{1,0:T(8,128)(2,1)S(1)}, u32[]{:S(2)}, u32[]{:S(2)}) collective-permute-start(bf16[512,512]{1,0:T(8,128)(2,1)S(1)} %bitcast.14), channel_id=1, source_target_pairs={{0,64},{64,128},{128,192},{192,0},{1,65},{65,129},{129,193},{193,1... | collective-permute-start | bytes 1572872 | tf_op jit(solution)/shard_map/ppermute | solution.py:416
  31.7 23.3 %collective-permute-start.1 = (bf16[512,512]{1,0:T(8,128)(2,1)S(1)}, bf16[512,512]{1,0:T(8,128)(2,1)S(1)}, u32[]{:S(2)}, u32[]{:S(2)}) collective-permute-start(bf16[512,512]{1,0:T(8,128)(2,1)S(1)} %bitcast.15), channel_id=1, source_target_pairs={{0,128},{64,192},{128,0},{192,64},{1,129},{65,193},{129,1},{193,65... | collective-permute-start | bytes 1572872 | tf_op jit(solution)/shard_map/ppermute | solution.py:416
  34.2 24.1 %collective-permute-start.2 = (bf16[512,512]{1,0:T(8,128)(2,1)S(1)}, bf16[512,512]{1,0:T(8,128)(2,1)S(1)}, u32[]{:S(2)}, u32[]{:S(2)}) collective-permute-start(bf16[512,512]{1,0:T(8,128)(2,1)S(1)} %bitcast.16), channel_id=1, source_target_pairs={{0,192},{64,0},{128,64},{192,128},{1,193},{65,1},{129,65},{193,129... | collective-permute-start | bytes 1572872 | tf_op jit(solution)/shard_map/ppermute | solution.py:416
  43.0 23.8 %all-to-all-start.1 = ((f32[32,4,512]{2,1,0:T(4,128)}), f32[32,4,512]{2,1,0:T(4,128)S(1)}, u32[]{:S(2)}, u32[]{:S(2)}) async-start(f32[32,4,512]{2,1,0:T(4,128)} %stats.1.pack_ref), calls=%async_computation.1 | async-start | bytes 524288 | tf_op jit(solution)/shard_map/all_to_all | solution.py:413
  49.5 17.3 %copy-start = (s32[512]{0:T(512)S(1)}, s32[512]{0:T(512)}, u32[]{:S(2)}) copy-start(s32[512]{0:T(512)} %param.6) | copy-start | bytes 6148
  49.5 33.4 %collective-permute-start.3 = (bf16[512,512]{1,0:T(8,128)(2,1)S(1)}, bf16[512,512]{1,0:T(8,128)(2,1)S(1)}, u32[]{:S(2)}, u32[]{:S(2)}) collective-permute-start(bf16[512,512]{1,0:T(8,128)(2,1)S(1)} %bitcast.19), channel_id=1, source_target_pairs={{0,32},{32,0},{1,33},{33,1},{2,34},{34,2},{3,35},{35,3},{4,36},{36... | collective-permute-start | bytes 1572872 | tf_op jit(solution)/shard_map/ppermute | solution.py:429
  52.2 30.7 %collective-permute-start.4 = (bf16[512,512]{1,0:T(8,128)(2,1)S(1)}, bf16[512,512]{1,0:T(8,128)(2,1)}, u32[]{:S(2)}, u32[]{:S(2)}) collective-permute-start(bf16[512,512]{1,0:T(8,128)(2,1)S(1)} %collective-permute-done.rest_1_), channel_id=1, source_target_pairs={{0,32},{32,0},{1,33},{33,1},{2,34},{34,2},{3,35},{35,3},{4,36},{36... | collective-permute-start | bytes 1572872 | tf_op jit(solution)/shard_map/ppermute | solution.py:429
  55.0 27.9 %collective-permute-start.5 = (bf16[512,512]{1,0:T(8,128)(2,1)S(1)}, bf16[512,512]{1,0:T(8,128)(2,1)}, u32[]{:S(2)}, u32[]{:S(2)}) collective-permute-start(bf16[512,512]{1,0:T(8,128)(2,1)S(1)} %collective-permute-done.1.rest_2_), channel_id=1, source_target_pairs={{0,32},{32,0},{1,33},{33,1},{2,34},{34,2},{3,35},{35,3},{4,36},{36... | collective-permute-start | bytes 1572872 | tf_op jit(solution)/shard_map/ppermute | solution.py:429
  58.3 24.7 %collective-permute-start.6 = (bf16[512,512]{1,0:T(8,128)(2,1)S(1)}, bf16[512,512]{1,0:T(8,128)(2,1)}, u32[]{:S(2)}, u32[]{:S(2)}) collective-permute-start(bf16[512,512]{1,0:T(8,128)(2,1)S(1)} %collective-permute-done.2.rest_3_), channel_id=1, source_target_pairs={{0,32},{32,0},{1,33},{33,1},{2,34},{34,2},{3,35},{35,3},{4,36},{36... | collective-permute-start | bytes 1572872 | tf_op jit(solution)/shard_map/ppermute | solution.py:429
  67.5 10.1 %all-to-all-start.2 = ((f32[8,4,512]{2,1,0:T(4,128)}), f32[8,4,512]{2,1,0:T(4,128)S(1)}, u32[]{:S(2)}, u32[]{:S(2)}) async-start(f32[8,4,512]{2,1,0:T(4,128)} %get-tuple-element.9.all_ref), calls=%async_computation.2 | async-start | bytes 131072 | tf_op jit(solution)/shard_map/all_to_all | solution.py:420
  77.6 18.5 %all-to-all-start.3 = ((bf16[32,16,256]{2,1,0:T(8,128)(2,1)}), bf16[32,16,256]{2,1,0:T(8,128)(2,1)S(1)}, u32[]{:S(2)}, u32[]{:S(2)}) async-start(bf16[32,16,256]{2,1,0:T(8,128)(2,1)} %bitcast.3), calls=%async_computation.3 | async-start | bytes 524288 | tf_op jit(solution)/shard_map/all_to_all | solution.py:423
